TPU v7x, 512 devices: a whole 4x8x8 slice. The times are simulated.
512 devices in a mesh: gx: 32 (over y, x), gy: 16 (over z, core).
Axes of the slice: x: 4, y: 8, z: 8, core: 2. Of those that a mesh axis runs over, the one named last changes fastest.
Arguments:
- hidden_in: bfloat16 [4096, 2560], P('gx'), may hold values from -48 to 48
- norm_gain: bfloat16 [2560], replicated, may hold values from 0.099609375 to 1.8984375
- router_weight: bfloat16 [2560, 64], replicated, may hold values from -3 to 3
- routes: int32 [4096, 6], P('gx'), may hold values from 0 to 63, as said below
- w_gate_up: bfloat16 [512, 2560, 384], P(('gx', 'gy')), may hold values from -0.125 to 0.125
- w_down: bfloat16 [512, 192, 2560], P(('gx', 'gy')), may hold values from -0.15625 to 0.15625
- final_gain: bfloat16 [2560], replicated, may hold values from 0.099609375 to 1.8984375
- head_weight: bfloat16 [2560, 53248], P('gy', 'gx'), may hold values from -5 to 5
- targets: int32 [4096], replicated, may hold values from 0 to 53247
Outputs:
- logprob: float32 [32, 128], P(None, 'gy')
- entropy: float32 [32, 128], P(None, 'gy')
Inputs may be any that keep to these rules, and one draw needn't show every extreme that they name: `routes`: each row names 6 different experts. Within the 128 rows of one index of gx no expert is named by more than 16 rows, and one expert, the same for every index of gx, is named by exactly 16 rows in each.
All inputs are finite; a program needn't handle non-finite values.
Results may differ from a plain program's by a relative error of at most 0.012.
Values may be sent and summed in bfloat16 or wider, within the bound.
A program may use at most 192 MiB of HBM per device.

v0:
```python
import jax
import jax.numpy as jnp
from jax import lax
from jax.sharding import PartitionSpec as P

SPLITS = 8
NORM_EPSILON = 1e-06


def rms_scale(values, gain_vector):
    widened = values.astype(jnp.float32)
    return (
        widened
        * lax.rsqrt(jnp.mean(widened * widened, -1, keepdims=True) + NORM_EPSILON)
        * gain_vector.astype(jnp.float32)
    )


def finish(peak_value, total_mass, spread, target_logit):
    log_mass = jnp.log(total_mass)
    return (target_logit - peak_value - log_mass, log_mass - spread / total_mass)


def shards(
    hidden_in, norm_gain, router_weight, routes, w_gate_up, w_down, final_gain, head_weight, targets
):
    tok_rows = hidden_in.shape[0]
    group_count = lax.axis_size("gx")
    lane_count = lax.axis_size("gy")
    group_index = lax.axis_index("gx")
    lane_index = lax.axis_index("gy")
    expert_count = router_weight.shape[1]
    held_slices = w_gate_up.shape[0]
    unit_count = w_down.shape[1]
    slot_count = tok_rows // 8
    share_rows = tok_rows // lane_count
    columns = head_weight.shape[1]
    normed = rms_scale(hidden_in, norm_gain).astype(jnp.bfloat16)
    scores = jnp.dot(normed, router_weight, preferred_element_type=jnp.float32)
    chosen = routes[:, :, None] == jnp.arange(expert_count, dtype=jnp.int32)[None, None, :]
    picked = jnp.sum(jnp.where(chosen, scores[:, None, :], 0.0), -1)
    gate_values = jax.nn.softmax(picked, axis=-1).astype(jnp.bfloat16)
    gate_table = jnp.sum(jnp.where(chosen, gate_values.astype(jnp.float32)[:, :, None], 0.0), 1)
    member = jnp.sum(chosen.astype(jnp.int32), 1)
    slot_rank = jnp.cumsum(member, 0) - member
    slot_hit = (member[:, :, None] == 1) & (
        slot_rank[:, :, None] == jnp.arange(slot_count, dtype=jnp.int32)[None, None, :]
    )
    lane_slices = (
        jnp.arange(group_count, dtype=jnp.int32)[:, None] * lane_count + lane_index
    ) * held_slices + jnp.arange(held_slices, dtype=jnp.int32)[None, :]
    owner_expert = lane_slices // SPLITS
    pick_expert = (
        owner_expert[:, :, None] == jnp.arange(expert_count, dtype=jnp.int32)[None, None, :]
    ).astype(jnp.bfloat16)
    dispatch = jnp.einsum(
        "tke,nec->tkcn",
        pick_expert,
        slot_hit.astype(jnp.bfloat16),
        preferred_element_type=jnp.float32,
    ).astype(jnp.bfloat16)
    outgoing = jnp.einsum(
        "tkcn,nd->tkcd", dispatch, normed, preferred_element_type=jnp.float32
    ).astype(jnp.bfloat16)
    expert_gate = jnp.einsum(
        "tke,ne->tkn",
        pick_expert,
        gate_table.astype(jnp.bfloat16),
        preferred_element_type=jnp.float32,
    )
    combine = (dispatch.astype(jnp.float32) * expert_gate[:, :, None, :]).astype(jnp.bfloat16)
    lifted = jnp.einsum(
        "skcd,kdf->skcf",
        lax.all_to_all(outgoing, "gx", split_axis=0, concat_axis=0, tiled=True),
        w_gate_up,
        preferred_element_type=jnp.float32,
    )
    active = (jax.nn.silu(lifted[..., :unit_count]) * lifted[..., unit_count:]).astype(jnp.bfloat16)
    result = jnp.einsum(
        "skcf,kfd->skcd", active, w_down, preferred_element_type=jnp.float32
    ).astype(jnp.bfloat16)
    returned = lax.all_to_all(result, "gx", split_axis=0, concat_axis=0, tiled=True)
    partial_value = jnp.einsum(
        "tkcn,tkcd->nd", combine, returned, preferred_element_type=jnp.float32
    )
    summed = lax.psum_scatter(partial_value, "gy", scatter_dimension=0, tiled=True)
    residual = lax.dynamic_slice_in_dim(hidden_in, lane_index * share_rows, share_rows, 0)
    layer_out = (residual.astype(jnp.float32) + summed).astype(jnp.bfloat16)
    final_states = rms_scale(layer_out, final_gain).astype(jnp.bfloat16)
    gathered = lax.all_gather(final_states, "gx", axis=0, tiled=True)
    target_grid = targets.reshape(group_count, tok_rows)
    logits = jnp.dot(
        gathered,
        lax.all_gather(head_weight, "gy", axis=0, tiled=True),
        preferred_element_type=jnp.float32,
    )
    offset = group_index * columns
    own_targets = lax.dynamic_slice_in_dim(
        target_grid, lane_index * share_rows, share_rows, 1
    ).reshape(group_count * share_rows)
    target_hits = (offset + jnp.arange(columns, dtype=jnp.int32))[None, :] == own_targets[:, None]
    peak_value = lax.pmax(jnp.max(logits, -1), "gx")
    shifted = logits - peak_value[:, None]
    weights = jnp.exp(shifted)
    total_mass, spread, target_logit = lax.psum(
        (
            jnp.sum(weights, -1),
            jnp.sum(weights * shifted, -1),
            jnp.sum(jnp.where(target_hits, logits, 0.0), -1),
        ),
        "gx",
    )
    logprob, entropy = finish(peak_value, total_mass, spread, target_logit)
    return (logprob.reshape(group_count, share_rows), entropy.reshape(group_count, share_rows))


def solution(mesh):
    return jax.shard_map(
        shards,
        mesh=mesh,
        in_specs=(
            P("gx", None),
            P(),
            P(),
            P("gx", None),
            P(("gx", "gy"), None, None),
            P(("gx", "gy"), None, None),
            P(),
            P("gy", "gx"),
            P(),
        ),
        out_specs=(P(None, "gy"), P(None, "gy")),
        check_vma=False,
    )
```

profile of v0, /device:TPU:2, one launch (start us, length us, event | category | flops | bytes accessed | tf_op | source)
XLA Modules:
  0.0 525.7 jit_solution(14808827266614481248)
XLA Ops:
  7.2 0.0 copy-start
  7.2 0.0 copy-start.1
  7.2 0.9 convert_reduce_fusion
  8.1 0.1 copy.35
  8.2 0.7 convert_element_type.89
  8.9 1.3 fusion.8
  10.2 0.2 reduce_window_sum.11
  10.4 0.1 copy.37
  10.4 0.3 convolution_convert_fusion.2
  10.7 0.0 copy-done.1
  10.7 0.9 fusion.1
  11.7 71.8 %all_to_all.10 = bf16[32,1,16,2560]{3,2,1,0:T(8,128)(2,1)S(1)} all-to-all(bf16[32,1,16,2560]{3,2,1,0:T(8,128)(2,1)S(1)} %fusion.1), channel_id=1, replica_groups=mesh['gx'=32,'gy'=16] {'gx'}, dimensions={0} | all-to-all | bytes 5242880 | tf_op jit(solution)/shard_map/all_to_all | solution.py:74
  83.5 0.0 copy-done
  83.5 0.0 copy-start.5
  83.5 1.5 fusion.11
  85.0 0.0 copy-done.5
  85.0 2.4 fusion
  87.5 0.0 copy-start.6
  87.5 5.8 %all-to-all-start.1 = ((bf16[32,1,16,2560]{3,2,1,0:T(8,128)(2,1)}), bf16[32,1,16,2560]{3,2,1,0:T(8,128)(2,1)}, u32[]{:S(2)}, u32[]{:S(2)}) async-start(bf16[32,1,16,2560]{3,2,1,0:T(8,128)(2,1)} %fusion), calls=%async_computation.1 | async-start | bytes 5242880 | tf_op jit(solution)/shard_map/all_to_all | solution.py:82
  93.3 0.0 reduce-scatter.2.cloned.1.call-start
  93.3 0.0 copy-done.6
  93.3 0.4 fusion.26
  93.8 0.0 copy-done.2
  93.9 0.2 fusion.36
  94.1 58.5 %all-to-all-done.1 = bf16[32,1,16,2560]{3,2,1,0:T(8,128)(2,1)} async-done(((bf16[32,1,16,2560]{3,2,1,0:T(8,128)(2,1)}), bf16[32,1,16,2560]{3,2,1,0:T(8,128)(2,1)}, u32[]{:S(2)}, u32[]{:S(2)}) %all-to-all-start.1) | async-done | bytes 2621472 | tf_op jit(solution)/shard_map/all_to_all | solution.py:82
  152.6 4.5 convolution_bitcast_fusion
  157.1 0.0 reduce-scatter.2.cloned.1.call-update
  157.1 0.0 all-gather.3.cloned.1.call-start
  157.2 0.0 copy-done.4
  157.2 62.9 %reduce-scatter.2.cloned.1.call-done = f32[8,2560]{1,0:T(8,128)} async-done(((f32[128,2560]{1,0:T(8,128)}), f32[8,2560]{1,0:T(8,128)}) %reduce-scatter.2.cloned.1.call-update) | async-done | bytes 81936 | tf_op jit(solution)/shard_map/reduce_scatter | solution.py:86
  220.1 1.0 fusion.33
  221.1 0.7 fusion.35
  221.8 0.0 all-gather.3.cloned.1.call-update
  221.8 0.0 all-gather.5.cloned.1.call-start
  221.9 0.7 all-gather.5.cloned.1.call-update
  222.6 0.0 copy-done.3
  222.6 0.1 constant_dynamic-slice_fusion
  222.7 0.1 eq.70
  222.8 79.2 %all-gather.3.cloned.1.call-done = bf16[256,2560]{1,0:T(8,128)(2,1)} async-done(((bf16[8,2560]{1,0:T(8,128)(2,1)}), bf16[256,2560]{1,0:T(8,128)(2,1)}) %all-gather.3.cloned.1.call-update) | async-done | bytes 1310736 | tf_op jit(solution)/shard_map/all_gather | solution.py:90
  301.9 61.2 %all-gather.5.cloned.1.call-done = bf16[2560,1664]{1,0:T(8,128)(2,1)} async-done(((bf16[160,1664]{1,0:T(8,128)(2,1)}), bf16[2560,1664]{1,0:T(8,128)(2,1)}) %all-gather.5.cloned.1.call-update) | async-done | bytes 8519696 | tf_op jit(solution)/shard_map/all_gather | solution.py:94
  363.1 7.6 %fusion.45 = (f32[256]{0:T(256)S(1)}, f32[256,1664]{1,0:T(8,128)}) fusion(bf16[256,2560]{1,0:T(8,128)(2,1)} %all-gather.3.cloned.1.call-done, bf16[2560,1664]{1,0:T(8,128)(2,1)} %all-gather.5.cloned.1.call-done), kind=kOutput, calls=%fused_computation.68 | convolution fusion | flops 2181463808 | bytes 11535360 | tf_op jit(solution)/shard_map/dot_general | solution.py:92
  370.7 70.6 %pmax.7 = f32[256]{0:T(256)S(1)} all-reduce(f32[256]{0:T(256)S(1)} %get-tuple-element.18), channel_id=1, replica_groups=mesh['gx'=32,'gy'=16] {'gx'}, use_global_device_ids=true, to_apply=%region_12.13 | all-reduce | flops 256 | bytes 2048 | tf_op jit(solution)/shard_map/pmax | solution.py:102
  441.4 2.1 fusion.7
  443.5 74.1 %all-reduce = (f32[256]{0:T(256)S(1)}, f32[256]{0:T(256)S(1)}, f32[256]{0:T(256)S(1)}) all-reduce(f32[256]{0:T(256)S(1)} %get-tuple-element.10, f32[256]{0:T(256)S(1)} %get-tuple-element.9, f32[256]{0:T(256)S(1)} %get-tuple-element.8), channel_id=1, replica_groups=mesh['gx'=32,'gy'=16] {'gx'}, use_global_device_ids=true, to_apply=%region_10.11 | all-reduce | flops 768 | bytes 6144 | tf_op jit(solution)/shard_map/psum | solution.py:105
  517.6 0.1 reshape.187
  517.7 0.7 copy.42
  518.4 0.1 reshape.188
  518.5 0.7 copy.43
  (16 shorter events, 0.2 us)
Async XLA Ops:
  7.2 76.3 %copy-start = (bf16[1,2560,384]{2,1,0:T(8,128)(2,1)S(1)}, bf16[1,2560,384]{2,1,0:T(8,128)(2,1)}, u32[]{:S(2)}) copy-start(bf16[1,2560,384]{2,1,0:T(8,128)(2,1)} %param.13) | copy-start | bytes 5898244
  7.2 3.5 copy-start.1
  83.5 1.5 copy-start.5
  87.5 5.8 %copy-start.6 = (bf16[2560,64]{0,1:T(8,128)(2,1)S(1)}, bf16[2560,64]{0,1:T(8,128)(2,1)}, u32[]{:S(2)}) copy-start(bf16[2560,64]{0,1:T(8,128)(2,1)} %param.11) | copy-start | bytes 983044
  87.5 6.3 %copy-start.2 = (s32[128,6]{0,1:T(8,128)S(1)}, s32[128,6]{0,1:T(8,128)}, u32[]{:S(2)}) copy-start(s32[128,6]{0,1:T(8,128)} %param.12) | copy-start | bytes 9220
  87.5 65.1 %all-to-all-start.1 = ((bf16[32,1,16,2560]{3,2,1,0:T(8,128)(2,1)}), bf16[32,1,16,2560]{3,2,1,0:T(8,128)(2,1)}, u32[]{:S(2)}, u32[]{:S(2)}) async-start(bf16[32,1,16,2560]{3,2,1,0:T(8,128)(2,1)} %fusion), calls=%async_computation.1 | async-start | bytes 5242880 | tf_op jit(solution)/shard_map/all_to_all | solution.py:82
  93.3 126.8 %reduce-scatter.2.cloned.1.call-start = ((), (), s32[]{:S(2)}) async-start(), calls=%async_computation.3 | async-start | bytes 1392640 | tf_op jit(solution)/shard_map/reduce_scatter | solution.py:86
  94.1 63.1 %copy-start.4 = (bf16[2560]{0:T(1024)(128)(2,1)S(1)}, bf16[2560]{0:T(1024)(128)(2,1)}, u32[]{:S(2)}) copy-start(bf16[2560]{0:T(1024)(128)(2,1)} %param.15) | copy-start | bytes 15364
  157.1 65.5 %copy-start.3 = (s32[4096]{0:T(1024)S(1)}, s32[4096]{0:T(1024)}, u32[]{:S(2)}) copy-start(s32[4096]{0:T(1024)} %param.17) | copy-start | bytes 49156
  157.1 144.8 %all-gather.3.cloned.1.call-start = ((), (), s32[]{:S(2)}) async-start(), calls=%async_computation.4 | async-start | bytes 1351680 | tf_op jit(solution)/shard_map/all_gather | solution.py:90
  221.8 141.3 %all-gather.5.cloned.1.call-start = ((), (), s32[]{:S(2)}) async-start(), calls=%async_computation.5 | async-start | bytes 9052160 | tf_op jit(solution)/shard_map/all_gather | solution.py:94
Sparse Core Ops, SparseCore 0:
  157.2 62.7 reduce-scatter.1
  223.2 78.6 all-gather.2
  304.1 59.0 all-gather.4
where the time goes:
time: 526 us
  waiting for transfers between devices  262 us (50%)
  blocking collectives  217 us (41%)
  matrix products  17.9 us (3%)
  between operations  13.9 us (3%)
  other arithmetic  7.05 us (1%)
  starting transfers between devices  5.9 us (1%)
    all_gather x1, waiting for transfers between devices, shards(): gathered = lax.all_gather(final_states, 'gx', axis=0, tiled=True)  79.2 us
    psum x1, blocking collectives, shards(): lax.psum((jnp.sum(weights, -1), jnp.sum(weights * shifted, -1), jnp.sum(j...  74.1 us
    all_to_all x1, blocking collectives, shards(): lax.all_to_all(outgoing, 'gx', split_axis=0, concat_axis=0, tiled=True)  71.8 us
    pmax x1, blocking collectives, shards(): peak_value = lax.pmax(jnp.max(logits, -1), 'gx')  70.6 us
    reduce_scatter x1, waiting for transfers between devices, shards(): lax.psum_scatter(partial_value, 'gy', scatter_dimension=0, tiled=True)  62.9 us
    all_gather x1, waiting for transfers between devices, shards(): lax.all_gather(head_weight, 'gy', axis=0, tiled=True)  61.2 us
    all_to_all x1, waiting for transfers between devices, shards(): lax.all_to_all(result, 'gx', split_axis=0, concat_axis=0, tiled=True)  58.5 us
  transfers between devices with their start and end apart: 4, of which 4 were waited for; matrix products, arithmetic and copies ran while one was open for 0% of the time, Pallas kernels for 0%

commit v1 on v0

--- a/solution.py
+++ b/solution.py
@@ -2,6 +2,7 @@
 import jax.numpy as jnp
 from jax import lax
 from jax.sharding import PartitionSpec as P
+from jax.lax import all_to_all, axis_size
 
 SPLITS = 8
 NORM_EPSILON = 1e-06
@@ -87,7 +88,10 @@
     residual = lax.dynamic_slice_in_dim(hidden_in, lane_index * share_rows, share_rows, 0)
     layer_out = (residual.astype(jnp.float32) + summed).astype(jnp.bfloat16)
     final_states = rms_scale(layer_out, final_gain).astype(jnp.bfloat16)
-    gathered = lax.all_gather(final_states, "gx", axis=0, tiled=True)
+    gathered = jnp.concatenate(
+        all_to_all(jnp.stack([final_states for _ in range(axis_size("gx"))], axis=0), "gx", 0, 0),
+        axis=0,
+    )
     target_grid = targets.reshape(group_count, tok_rows)
     logits = jnp.dot(
         gathered,

time: 526 us -> 443 us (0.84)
  waiting for transfers between devices: 262 us -> 169 us
  starting transfers between devices: 5.9 us -> 15.8 us
    all_gather x1 -> x0, waiting for transfers between devices: 79.2 us -> none  [shards(): gathered = lax.all_gather(final_states, 'gx', axis=0, tiled=True)]
    all_gather x1, waiting for transfers between devices: 61.2 us -> 17.3 us  [shards(): lax.all_gather(head_weight, 'gy', axis=0, tiled=True)]
    all_to_all x0 -> x1, waiting for transfers between devices: none -> 30.2 us  [shards(): all_to_all(jnp.stack([final_states for _ in range(axis_size('gx'))], axis...]
    all_to_all x0 -> x1, starting transfers between devices: none -> 9.93 us  [shards(): all_to_all(jnp.stack([final_states for _ in range(axis_size('gx'))], axis...]
  transfers between devices with their start and end apart: 4 -> 4, of which waited for: 4 -> 4; matrix products, arithmetic and copies ran while one was open for 0% -> 1% of each run, Pallas kernels for 0% -> 0%
where the time goes in v1:
time: 443 us
  blocking collectives  217 us (49%)
  waiting for transfers between devices  169 us (38%)
  matrix products  17.9 us (4%)
  starting transfers between devices  15.8 us (4%)
  between operations  14.2 us (3%)
  other arithmetic  6.43 us (1%)
    psum x1, blocking collectives, shards(): lax.psum((jnp.sum(weights, -1), jnp.sum(weights * shifted, -1), jnp.sum(j...  74.1 us
    all_to_all x1, blocking collectives, shards(): lax.all_to_all(outgoing, 'gx', split_axis=0, concat_axis=0, tiled=True)  71.8 us
    pmax x1, blocking collectives, shards(): peak_value = lax.pmax(jnp.max(logits, -1), 'gx')  70.6 us
    reduce_scatter x1, waiting for transfers between devices, shards(): lax.psum_scatter(partial_value, 'gy', scatter_dimension=0, tiled=True)  62.2 us
    all_to_all x1, waiting for transfers between devices, shards(): lax.all_to_all(result, 'gx', split_axis=0, concat_axis=0, tiled=True)  58.5 us
    all_to_all x1, waiting for transfers between devices, shards(): all_to_all(jnp.stack([final_states for _ in range(axis_size('gx'))], axis...  30.2 us
    all_gather x1, waiting for transfers between devices, shards(): lax.all_gather(head_weight, 'gy', axis=0, tiled=True)  17.3 us
    all_to_all x1, starting transfers between devices, shards(): all_to_all(jnp.stack([final_states for _ in range(axis_size('gx'))], axis...  9.93 us
  transfers between devices with their start and end apart: 4, of which 4 were waited for; matrix products, arithmetic and copies ran while one was open for 1% of the time, Pallas kernels for 0%

profile of v1, /device:TPU:2, one launch (start us, length us, event | category | flops | bytes accessed | tf_op | source)
XLA Modules:
  0.0 442.9 jit_solution(2619498923444398972)
XLA Ops:
  7.2 0.0 copy-start
  7.2 0.0 copy-start.1
  7.2 0.9 convert_reduce_fusion
  8.1 0.1 copy.35
  8.2 0.7 convert_element_type.89
  8.9 1.3 fusion.8
  10.2 0.2 reduce_window_sum.11
  10.4 0.1 copy.37
  10.4 0.3 convolution_convert_fusion.2
  10.7 0.0 copy-done.1
  10.7 0.9 fusion.1
  11.7 71.8 %all_to_all.15 = bf16[32,1,16,2560]{3,2,1,0:T(8,128)(2,1)S(1)} all-to-all(bf16[32,1,16,2560]{3,2,1,0:T(8,128)(2,1)S(1)} %fusion.1), channel_id=1, replica_groups=mesh['gx'=32,'gy'=16] {'gx'}, dimensions={0} | all-to-all | bytes 5242880 | tf_op jit(solution)/shard_map/all_to_all | solution.py:75
  83.5 0.0 copy-done
  83.5 0.0 copy-start.5
  83.5 1.5 fusion.13
  85.0 0.0 copy-done.5
  85.0 2.4 fusion
  87.5 5.8 %all-to-all-start.1 = ((bf16[32,1,16,2560]{3,2,1,0:T(8,128)(2,1)}), bf16[32,1,16,2560]{3,2,1,0:T(8,128)(2,1)}, u32[]{:S(2)}, u32[]{:S(2)}) async-start(bf16[32,1,16,2560]{3,2,1,0:T(8,128)(2,1)} %fusion), calls=%async_computation.1 | async-start | bytes 5242880 | tf_op jit(solution)/shard_map/all_to_all | solution.py:83
  93.3 0.0 reduce-scatter.2.cloned.1.call-start
  93.3 0.0 copy-done.6
  93.3 0.4 fusion.28
  93.8 0.0 copy-done.2
  93.9 0.2 fusion.38
  94.1 58.5 %all-to-all-done.1 = bf16[32,1,16,2560]{3,2,1,0:T(8,128)(2,1)} async-done(((bf16[32,1,16,2560]{3,2,1,0:T(8,128)(2,1)}), bf16[32,1,16,2560]{3,2,1,0:T(8,128)(2,1)}, u32[]{:S(2)}, u32[]{:S(2)}) %all-to-all-start.1) | async-done | bytes 2621472 | tf_op jit(solution)/shard_map/all_to_all | solution.py:83
  152.6 4.6 %convolution_bitcast_fusion = f32[128,2560]{1,0:T(8,128)} fusion(bf16[32,1,16,2560]{3,2,1,0:T(8,128)(2,1)} %all-to-all-done.1, bf16[128,16,32]{0,2,1:T(8,128)(2,1)S(1)} %convolution_convert_fusion.2, f32[32,128]{1,0:T(8,128)S(1)} %fusion.38), kind=kOutput, calls=%fused_computation.4 | convolution fusion | flops 335740928 | bytes 4079616 | tf_op jit(solution)/shard_map/tkcn,tkcd->nd/dot_general | solution.py:84
  157.1 0.0 reduce-scatter.2.cloned.1.call-update
  157.2 0.0 all-gather.2.cloned.1.call-start
  157.2 0.7 all-gather.2.cloned.1.call-update
  157.9 0.0 copy-done.4
  157.9 62.2 %reduce-scatter.2.cloned.1.call-done = f32[8,2560]{1,0:T(8,128)} async-done(((f32[128,2560]{1,0:T(8,128)}), f32[8,2560]{1,0:T(8,128)}) %reduce-scatter.2.cloned.1.call-update) | async-done | bytes 81936 | tf_op jit(solution)/shard_map/reduce_scatter | solution.py:87
  220.1 1.0 fusion.35
  221.2 0.1 fusion.37
  221.2 0.0 copy-start.3
  221.3 1.2 stack.2
  222.5 9.9 %all-to-all-start.2 = ((bf16[32,8,2560]{2,1,0:T(8,128)(2,1)}), bf16[32,8,2560]{2,1,0:T(8,128)(2,1)}, u32[]{:S(2)}, u32[]{:S(2)}) async-start(bf16[32,8,2560]{2,1,0:T(8,128)(2,1)} %stack.2), calls=%async_computation.3 | async-start | bytes 2621440 | tf_op jit(solution)/shard_map/all_to_all | solution.py:92
  232.4 0.0 copy-done.3
  232.4 0.1 constant_dynamic-slice_fusion
  232.5 0.1 eq.70
  232.6 30.2 %all-to-all-done.2 = bf16[32,8,2560]{2,1,0:T(8,128)(2,1)} async-done(((bf16[32,8,2560]{2,1,0:T(8,128)(2,1)}), bf16[32,8,2560]{2,1,0:T(8,128)(2,1)}, u32[]{:S(2)}, u32[]{:S(2)}) %all-to-all-start.2) | async-done | bytes 1310752 | tf_op jit(solution)/shard_map/all_to_all | solution.py:92
  262.8 17.3 %all-gather.2.cloned.1.call-done = bf16[2560,1664]{1,0:T(8,128)(2,1)} async-done(((bf16[160,1664]{1,0:T(8,128)(2,1)}), bf16[2560,1664]{1,0:T(8,128)(2,1)}) %all-gather.2.cloned.1.call-update) | async-done | bytes 8519696 | tf_op jit(solution)/shard_map/all_gather | solution.py:98
  280.1 7.6 %fusion.47 = (f32[256]{0:T(256)S(1)}, f32[256,1664]{1,0:T(8,128)}) fusion(bf16[2560,1664]{1,0:T(8,128)(2,1)} %all-gather.2.cloned.1.call-done, bf16[32,8,2560]{2,1,0:T(8,128)(2,1)} %all-to-all-done.2), kind=kOutput, calls=%fused_computation.70 | convolution fusion | flops 2181463808 | bytes 11535360 | tf_op jit(solution)/shard_map/dot_general | solution.py:96
  287.7 70.6 %pmax.7 = f32[256]{0:T(256)S(1)} all-reduce(f32[256]{0:T(256)S(1)} %get-tuple-element.18), channel_id=1, replica_groups=mesh['gx'=32,'gy'=16] {'gx'}, use_global_device_ids=true, to_apply=%region_12.13 | all-reduce | flops 256 | bytes 2048 | tf_op jit(solution)/shard_map/pmax | solution.py:106
  358.3 2.1 fusion.7
  360.4 74.1 %all-reduce = (f32[256]{0:T(256)S(1)}, f32[256]{0:T(256)S(1)}, f32[256]{0:T(256)S(1)}) all-reduce(f32[256]{0:T(256)S(1)} %get-tuple-element.10, f32[256]{0:T(256)S(1)} %get-tuple-element.9, f32[256]{0:T(256)S(1)} %get-tuple-element.8), channel_id=1, replica_groups=mesh['gx'=32,'gy'=16] {'gx'}, use_global_device_ids=true, to_apply=%region_10.11 | all-reduce | flops 768 | bytes 6144 | tf_op jit(solution)/shard_map/psum | solution.py:109
  434.6 0.1 reshape.193
  434.7 0.7 copy.42
  435.3 0.1 reshape.194
  435.4 0.7 copy.43
  (16 shorter events, 0.2 us)
Async XLA Ops:
  7.2 76.3 %copy-start = (bf16[1,2560,384]{2,1,0:T(8,128)(2,1)S(1)}, bf16[1,2560,384]{2,1,0:T(8,128)(2,1)}, u32[]{:S(2)}) copy-start(bf16[1,2560,384]{2,1,0:T(8,128)(2,1)} %param.13) | copy-start | bytes 5898244
  7.2 3.5 copy-start.1
  83.5 1.5 copy-start.5
  87.5 5.8 %copy-start.6 = (bf16[2560,64]{0,1:T(8,128)(2,1)S(1)}, bf16[2560,64]{0,1:T(8,128)(2,1)}, u32[]{:S(2)}) copy-start(bf16[2560,64]{0,1:T(8,128)(2,1)} %param.11) | copy-start | bytes 983044
  87.5 6.3 %copy-start.2 = (s32[128,6]{0,1:T(8,128)S(1)}, s32[128,6]{0,1:T(8,128)}, u32[]{:S(2)}) copy-start(s32[128,6]{0,1:T(8,128)} %param.12) | copy-start | bytes 9220
  87.5 65.1 %all-to-all-start.1 = ((bf16[32,1,16,2560]{3,2,1,0:T(8,128)(2,1)}), bf16[32,1,16,2560]{3,2,1,0:T(8,128)(2,1)}, u32[]{:S(2)}, u32[]{:S(2)}) async-start(bf16[32,1,16,2560]{3,2,1,0:T(8,128)(2,1)} %fusion), calls=%async_computation.1 | async-start | bytes 5242880 | tf_op jit(solution)/shard_map/all_to_all | solution.py:83
  93.3 126.9 %reduce-scatter.2.cloned.1.call-start = ((), (), s32[]{:S(2)}) async-start(), calls=%async_computation.4 | async-start | bytes 1392640 | tf_op jit(solution)/shard_map/reduce_scatter | solution.py:87
  157.1 0.8 copy-start.4
  157.2 122.9 %all-gather.2.cloned.1.call-start = ((), (), s32[]{:S(2)}) async-start(), calls=%async_computation.5 | async-start | bytes 9052160 | tf_op jit(solution)/shard_map/all_gather | solution.py:98
  221.2 11.2 %copy-start.3 = (s32[4096]{0:T(1024)S(1)}, s32[4096]{0:T(1024)}, u32[]{:S(2)}) copy-start(s32[4096]{0:T(1024)} %param.17) | copy-start | bytes 49156
  222.5 40.3 %all-to-all-start.2 = ((bf16[32,8,2560]{2,1,0:T(8,128)(2,1)}), bf16[32,8,2560]{2,1,0:T(8,128)(2,1)}, u32[]{:S(2)}, u32[]{:S(2)}) async-start(bf16[32,8,2560]{2,1,0:T(8,128)(2,1)} %stack.2), calls=%async_computation.3 | async-start | bytes 2621440 | tf_op jit(solution)/shard_map/all_to_all | solution.py:92
Sparse Core Ops, SparseCore 0:
  157.3 62.7 reduce-scatter.1
  222.2 57.7 all-gather.1
